TPU v7x, 128 devices: a whole 4x4x4 slice. The times are simulated.
128 devices in a mesh: rows: 8 (over z, core), cols: 16 (over y, x).
Axes of the slice: x: 4, y: 4, z: 4, core: 2. Of those that a mesh axis runs over, the one named last changes fastest.
Arguments:
- pivot_rhs: float32 [4, 4096, 1024], P(None, 'cols'), may hold values from -6 to 6
- bound_sol: bfloat16 [16384, 1024], P('rows'), may hold values from -6 to 6
- border_tiles: bfloat16 [16384, 4, 4096], P('rows', None, 'cols'), may hold values from -0.046875 to 0.046875
- lower_tiles: bfloat16 [6, 4096, 4096], P(None, 'rows', 'cols'), may hold values from -0.09375 to 0.09375
- inverse_diag: bfloat16 [4, 4096, 4096], P(None, 'cols', 'rows'), may hold values from -0.09375 to 0.09375
- owner_map: int32 [128, 128, 1], P(('rows', 'cols')), may hold values from 0 to 127; in each aligned block of 128 rows (0 to 127, 128 to 255, ..., all dimensions but the last counted through in order) at most 2 rows name the same one
Outputs:
- child_rows: float32 [32768, 1024], P(('rows', 'cols'))
Inputs may be any that keep to these rules, and one draw needn't show every extreme that they name: `owner_map`: among the rows of one device (one index of the first dimension), no owner is named more than 2 times, a bound that some block reaches; every owner is named somewhere.
All inputs are finite; a program needn't handle non-finite values.
Results may differ from a plain program's by a relative error of at most 0.008.
Values may be sent and summed in bfloat16 or wider, within the bound.
No kernel may reach another device: no remote copies, remote signals or barrier semaphores. Data moves between devices by JAX's collectives and lax.ppermute only.
A program may use at most 64 MiB of HBM per device.

v0:
```python
import jax
import jax.numpy as jnp
from jax import lax
from jax.sharding import PartitionSpec as P


def pair_slot(later, earlier):
    return later * (later - 1) // 2 + earlier


def pack_rows(rows_here, owners, devices, most):
    onehot = (owners[:, None] == jnp.arange(devices, dtype=jnp.int32)[None, :]).astype(jnp.int32)
    ranks = jnp.cumsum(onehot, axis=0) - onehot
    slots = jnp.sum(ranks * onehot, axis=1)
    target = owners * most + slots
    select = (jnp.arange(devices * most, dtype=jnp.int32)[:, None] == target[None, :]).astype(
        jnp.float32
    )
    return jnp.dot(
        select, rows_here, precision=lax.Precision.HIGHEST, preferred_element_type=jnp.float32
    )


def tile_term(tile, vectors):
    return lax.dot_general(
        tile, vectors, (((0,), (0,)), ((), ())), preferred_element_type=jnp.float32
    )


def local(pivot_rhs, bound_sol, border_tiles, lower_tiles, inverse_diag, owner_map):
    devices = lax.axis_size("rows") * lax.axis_size("cols")
    blocks = pivot_rhs.shape[0]
    width_here = pivot_rhs.shape[1]
    sources = pivot_rhs.shape[2]
    rows_dev = owner_map.shape[1]
    most = max(2, 2 * rows_dev // devices)
    border_part = lax.dot_general(
        border_tiles, bound_sol, (((0,), (0,)), ((), ())), preferred_element_type=jnp.float32
    )
    pending = []
    border_full = lax.psum(border_part, "rows")
    for k in range(blocks):
        pending.append(jnp.zeros((width_here, sources), jnp.float32))
    rounded = [None] * blocks
    own_rows = [None] * blocks
    for k in reversed(range(blocks)):
        local_sum = pending[k]
        for j in range(k + 1, blocks):
            local_sum = local_sum + tile_term(lower_tiles[pair_slot(j, k)], rounded[j])
        summed = lax.psum(local_sum, "rows")
        summed = summed + border_full[k]
        residual = (pivot_rhs[k] - summed).astype(jnp.bfloat16)
        inverse_here = inverse_diag[k]
        solved_here = lax.psum_scatter(
            tile_term(inverse_here, residual), "cols", scatter_dimension=0, tiled=True
        )
        own_rows[k] = solved_here
        if k > 0:
            rounded[k] = lax.all_gather(
                solved_here.astype(jnp.bfloat16), "cols", axis=0, tiled=True
            )
    rows_here = jnp.concatenate(own_rows, axis=0)
    owners = owner_map[0, :, 0]
    buffer = pack_rows(rows_here, owners, devices, most).reshape(devices, most, sources)
    received = lax.all_to_all(buffer, ("rows", "cols"), split_axis=0, concat_axis=0, tiled=True)
    return received.reshape(devices * most, sources)


def solution(mesh):
    placed = (
        P(None, "cols", None),
        P("rows", None),
        P("rows", None, "cols"),
        P(None, "rows", "cols"),
        P(None, "cols", "rows"),
        P(("rows", "cols"), None, None),
    )
    return jax.shard_map(
        local, mesh=mesh, in_specs=placed, out_specs=P(("rows", "cols"), None), check_vma=False
    )
```

profile of v0, /device:TPU:1, one launch (start us, length us, event | category | flops | bytes accessed | tf_op | source)
XLA Modules:
  0.0 773.4 jit_solution(16388644528442897463)
XLA Ops:
  6.5 10.0 %fusion = f32[4,256,1024]{2,1,0:T(8,128)} fusion(bf16[2048,1024]{1,0:T(8,128)(2,1)} %param.7, bf16[2048,4,256]{2,1,0:T(4,128)(2,1)} %param.8), kind=kOutput, calls=%fused_computation | convolution fusion | flops 4294967296 | bytes 12582912 | tf_op jit(solution)/shard_map/dot_general | solution.py:37
  16.6 74.5 %all-reduce.5.cloned.1.call-done = f32[4,256,1024]{2,1,0:T(8,128)} async-done(((f32[4,256,1024]{2,1,0:T(8,128)}), f32[4,256,1024]{2,1,0:T(8,128)}) %all-reduce.5.cloned.1.call-update) | async-done | bytes 4194320 | tf_op jit(solution)/shard_map/psum | solution.py:41
  91.2 2.1 convolution_bitcast_fusion.3
  93.2 1.8 copy.28
  95.1 74.3 %reduce-scatter.13.cloned.1.call-done = f32[32,1024]{1,0:T(8,128)} async-done(((f32[512,1024]{1,0:T(8,128)}), f32[32,1024]{1,0:T(8,128)}) %reduce-scatter.13.cloned.1.call-update) | async-done | bytes 131088 | tf_op jit(solution)/shard_map/reduce_scatter | solution.py:54
  169.5 1.5 convert_element_type.31
  171.1 42.9 %all-gather.4.cloned.1.call-done = bf16[512,1024]{1,0:T(8,128)(2,1)} async-done(((bf16[32,1024]{1,0:T(8,128)(2,1)}), bf16[512,1024]{1,0:T(8,128)(2,1)}) %all-gather.4.cloned.1.call-update) | async-done | bytes 1048592 | tf_op jit(solution)/shard_map/all_gather | solution.py:59
  214.0 2.7 convolution_bitcast_fusion.4
  216.8 61.5 %all-reduce.7.cloned.1.call-done = f32[256,1024]{1,0:T(8,128)} async-done(((f32[256,1024]{1,0:T(8,128)}), f32[256,1024]{1,0:T(8,128)}) %all-reduce.7.cloned.1.call-update) | async-done | bytes 1048592 | tf_op jit(solution)/shard_map/psum | solution.py:50
  278.3 2.5 convolution_bitcast_fusion.2
  280.8 1.8 copy.30
  282.7 73.8 %reduce-scatter.15.cloned.1.call-done = f32[32,1024]{1,0:T(8,128)} async-done(((f32[512,1024]{1,0:T(8,128)}), f32[32,1024]{1,0:T(8,128)}) %reduce-scatter.15.cloned.1.call-update) | async-done | bytes 131088 | tf_op jit(solution)/shard_map/reduce_scatter | solution.py:54
  356.5 1.5 convert_element_type.33
  358.1 42.5 %all-gather.6.cloned.1.call-done = bf16[512,1024]{1,0:T(8,128)(2,1)} async-done(((bf16[32,1024]{1,0:T(8,128)(2,1)}), bf16[512,1024]{1,0:T(8,128)(2,1)}) %all-gather.6.cloned.1.call-update) | async-done | bytes 1048592 | tf_op jit(solution)/shard_map/all_gather | solution.py:59
  400.6 1.7 fusion.35
  402.4 2.4 fusion.4
  404.9 61.5 %all-reduce.9.cloned.1.call-done = f32[256,1024]{1,0:T(8,128)} async-done(((f32[256,1024]{1,0:T(8,128)}), f32[256,1024]{1,0:T(8,128)}) %all-reduce.9.cloned.1.call-update) | async-done | bytes 1048592 | tf_op jit(solution)/shard_map/psum | solution.py:50
  466.4 2.5 convolution_bitcast_fusion.1
  468.8 1.8 copy.32
  470.8 73.8 %reduce-scatter.17.cloned.1.call-done = f32[32,1024]{1,0:T(8,128)} async-done(((f32[512,1024]{1,0:T(8,128)}), f32[32,1024]{1,0:T(8,128)}) %reduce-scatter.17.cloned.1.call-update) | async-done | bytes 131088 | tf_op jit(solution)/shard_map/reduce_scatter | solution.py:54
  544.6 1.5 convert_element_type.35
  546.2 42.9 %all-gather.8.cloned.1.call-done = bf16[512,1024]{1,0:T(8,128)(2,1)} async-done(((bf16[32,1024]{1,0:T(8,128)(2,1)}), bf16[512,1024]{1,0:T(8,128)(2,1)}) %all-gather.8.cloned.1.call-update) | async-done | bytes 1048592 | tf_op jit(solution)/shard_map/all_gather | solution.py:59
  589.1 1.7 fusion.31
  590.8 1.4 convolution_add_fusion.1
  592.3 2.4 fusion.3
  595.0 61.3 %all-reduce.11.cloned.1.call-done = f32[256,1024]{1,0:T(8,128)} async-done(((f32[256,1024]{1,0:T(8,128)}), f32[256,1024]{1,0:T(8,128)}) %all-reduce.11.cloned.1.call-update) | async-done | bytes 1048592 | tf_op jit(solution)/shard_map/psum | solution.py:50
  656.3 2.5 convolution_bitcast_fusion
  658.8 1.9 copy.34
  661.8 72.8 %reduce-scatter.19.cloned.1.call-done = f32[32,1024]{1,0:T(8,128)} async-done(((f32[512,1024]{1,0:T(8,128)}), f32[32,1024]{1,0:T(8,128)}) %reduce-scatter.19.cloned.1.call-update) | async-done | bytes 131088
  734.6 1.1 copy.35
  737.3 27.9 %all_to_all.5 = f32[128,2,1024]{2,1,0:T(2,128)S(1)} all-to-all(f32[128,2,1024]{2,1,0:T(2,128)S(1)} %reshape.16), channel_id=1, replica_groups=mesh['rows'=8,'cols'=16] {'rows','cols'}, dimensions={0} | all-to-all | bytes 2097152 | tf_op jit(solution)/shard_map/all_to_all | solution.py:65
  765.2 1.7 reshape.17
  (43 shorter events, 3.4 us)
Async XLA Ops:
  6.5 84.6 %all-reduce.5.cloned.1.call-start = ((), (), s32[]{:S(2)}) async-start(), calls=%async_computation.5 | async-start | bytes 8388608 | tf_op jit(solution)/shard_map/psum | solution.py:41
  16.6 152.9 %reduce-scatter.13.cloned.1.call-start = ((), (), s32[]{:S(2)}) async-start(), calls=%async_computation.12 | async-start | bytes 2228224 | tf_op jit(solution)/shard_map/reduce_scatter | solution.py:54
  95.1 118.9 %all-gather.4.cloned.1.call-start = ((), (), s32[]{:S(2)}) async-start(), calls=%async_computation.6 | async-start | bytes 1114112 | tf_op jit(solution)/shard_map/all_gather | solution.py:59
  171.0 107.3 %all-reduce.7.cloned.1.call-start = ((), (), s32[]{:S(2)}) async-start(), calls=%async_computation.7 | async-start | bytes 2097152 | tf_op jit(solution)/shard_map/psum | solution.py:50
  216.7 139.7 %reduce-scatter.15.cloned.1.call-start = ((), (), s32[]{:S(2)}) async-start(), calls=%async_computation.13 | async-start | bytes 2228224 | tf_op jit(solution)/shard_map/reduce_scatter | solution.py:54
  280.8 121.6 %copy-start = (bf16[512,1024]{1,0:T(8,128)(2,1)S(1)}, bf16[512,1024]{1,0:T(8,128)(2,1)}, u32[]{:S(2)}) copy-start(bf16[512,1024]{1,0:T(8,128)(2,1)} %all-gather.4.cloned.1.call-done) | copy-start | bytes 3145732
  282.6 118.0 %all-gather.6.cloned.1.call-start = ((), (), s32[]{:S(2)}) async-start(), calls=%async_computation.8 | async-start | bytes 1114112 | tf_op jit(solution)/shard_map/all_gather | solution.py:59
  358.0 108.3 %all-reduce.9.cloned.1.call-start = ((), (), s32[]{:S(2)}) async-start(), calls=%async_computation.9 | async-start | bytes 2097152 | tf_op jit(solution)/shard_map/psum | solution.py:50
  404.8 139.7 %reduce-scatter.17.cloned.1.call-start = ((), (), s32[]{:S(2)}) async-start(), calls=%async_computation.14 | async-start | bytes 2228224 | tf_op jit(solution)/shard_map/reduce_scatter | solution.py:54
  470.7 120.1 %copy-start.1 = (bf16[512,1024]{1,0:T(8,128)(2,1)S(1)}, bf16[512,1024]{1,0:T(8,128)(2,1)}, u32[]{:S(2)}) copy-start(bf16[512,1024]{1,0:T(8,128)(2,1)} %all-gather.6.cloned.1.call-done) | copy-start | bytes 3145732
  470.7 118.4 %all-gather.8.cloned.1.call-start = ((), (), s32[]{:S(2)}) async-start(), calls=%async_computation.10 | async-start | bytes 1114112 | tf_op jit(solution)/shard_map/all_gather | solution.py:59
  546.1 110.1 %all-reduce.11.cloned.1.call-start = ((), (), s32[]{:S(2)}) async-start(), calls=%async_computation.11 | async-start | bytes 2097152 | tf_op jit(solution)/shard_map/psum | solution.py:50
  594.7 139.9 %reduce-scatter.19.cloned.1.call-start = ((), (), s32[]{:S(2)}) async-start(), calls=%async_computation.15 | async-start | bytes 2228224
  658.8 1.9 copy-start.5
  658.8 2.4 copy-start.2
  658.8 2.6 copy-start.3
  658.8 2.8 copy-start.4
Sparse Core Ops, SparseCore 0:
  16.7 74.4 all-reduce.4
  95.2 74.1 reduce-scatter.12
  171.8 42.1 all-gather.3
  216.9 61.3 all-reduce.6
  282.8 73.6 reduce-scatter.14
  358.5 42.1 all-gather.5
  404.9 61.3 all-reduce.8
  470.8 73.6 reduce-scatter.16
  546.9 42.0 all-gather.7
  594.8 61.3 all-reduce.10
  660.8 73.7 reduce-scatter.18
where the time goes:
time: 774 us; the launch traced here: 773 us
  waiting for transfers between devices  682 us (88%)
  matrix products  33 us (4%)
  blocking collectives  27.9 us (4%)
  between operations  13.4 us (2%)
  local copies, waits for them, and re-layouts  11.4 us (1%)
    reduce_scatter x3, waiting for transfers between devices, local(): lax.psum_scatter(tile_term(inverse_here, residual), 'cols', scatter_dimen...  222 us
    psum x3, waiting for transfers between devices, local(): summed = lax.psum(local_sum, 'rows')  184 us
    all_gather x3, waiting for transfers between devices, local(): lax.all_gather(solved_here.astype(jnp.bfloat16), 'cols', axis=0, tiled=True)  128 us
    psum x1, waiting for transfers between devices, local(): border_full = lax.psum(border_part, 'rows')  74.5 us
    unnamed x12, waiting for transfers between devices  73 us
    all_to_all x1, blocking collectives, local(): lax.all_to_all(buffer, ('rows', 'cols'), split_axis=0, concat_axis=0, til...  27.9 us
    dot_general x10, matrix products, tile_term(): lax.dot_general(tile, vectors, (((0,), (0,)), ((), ())), preferred_elemen...  22 us
  transfers between devices with their start and end apart: 11, of which 11 were waited for; matrix products, arithmetic and copies ran while one was open for 0% of the time, Pallas kernels for 0%

commit v1 on v0

--- a/solution.py
+++ b/solution.py
@@ -56,8 +56,14 @@
         )
         own_rows[k] = solved_here
         if k > 0:
-            rounded[k] = lax.all_gather(
-                solved_here.astype(jnp.bfloat16), "cols", axis=0, tiled=True
+            rounded[k] = jnp.concatenate(
+                lax.all_to_all(
+                    jnp.stack([solved_here.astype(jnp.bfloat16)] * lax.axis_size("cols")),
+                    "cols",
+                    0,
+                    0,
+                ),
+                axis=0,
             )
     rows_here = jnp.concatenate(own_rows, axis=0)
     owners = owner_map[0, :, 0]

time: 774 us -> 701 us (0.906)
  waiting for transfers between devices: 682 us -> 554 us
  blocking collectives: 27.9 us -> 83 us
    all_gather x3 -> x0, waiting for transfers between devices: 128 us -> none  [local(): lax.all_gather(solved_here.astype(jnp.bfloat16), 'cols', axis=0, tiled=True)]
    all_to_all x0 -> x3, blocking collectives: none -> 55.2 us  [local(): lax.all_to_all(jnp.stack([solved_here.astype(jnp.bfloat16)] * lax.axis_si...]
    unnamed x12 -> x9, waiting for transfers between devices: 73 us -> 72.9 us
  transfers between devices with their start and end apart: 11 -> 8, of which waited for: 11 -> 8; matrix products, arithmetic and copies ran while one was open for 0% -> 0% of each run, Pallas kernels for 0% -> 0%
where the time goes in v1:
time: 701 us
  waiting for transfers between devices  554 us (79%)
  blocking collectives  83 us (12%)
  matrix products  33.3 us (5%)
  between operations  13.7 us (2%)
  local copies, waits for them, and re-layouts  12.9 us (2%)
    reduce_scatter x3, waiting for transfers between devices, local(): lax.psum_scatter(tile_term(inverse_here, residual), 'cols', scatter_dimen...  222 us
    psum x3, waiting for transfers between devices, local(): summed = lax.psum(local_sum, 'rows')  185 us
    psum x1, waiting for transfers between devices, local(): border_full = lax.psum(border_part, 'rows')  74.5 us
    unnamed x9, waiting for transfers between devices  72.9 us
    all_to_all x3, blocking collectives, local(): lax.all_to_all(jnp.stack([solved_here.astype(jnp.bfloat16)] * lax.axis_si...  55.2 us
    all_to_all x1, blocking collectives, local(): lax.all_to_all(buffer, ('rows', 'cols'), split_axis=0, concat_axis=0, til...  27.9 us
    dot_general x10, matrix products, tile_term(): lax.dot_general(tile, vectors, (((0,), (0,)), ((), ())), preferred_elemen...  22.3 us
  transfers between devices with their start and end apart: 8, of which 8 were waited for; matrix products, arithmetic and copies ran while one was open for 0% of the time, Pallas kernels for 0%

profile of v1, /device:TPU:1, one launch (start us, length us, event | category | flops | bytes accessed | tf_op | source)
XLA Modules:
  0.0 700.8 jit_solution(11687962205961455212)
XLA Ops:
  6.5 10.0 %fusion = f32[4,256,1024]{2,1,0:T(8,128)} fusion(bf16[2048,1024]{1,0:T(8,128)(2,1)} %param.7, bf16[2048,4,256]{2,1,0:T(4,128)(2,1)} %param.8), kind=kOutput, calls=%fused_computation | convolution fusion | flops 4294967296 | bytes 12582912 | tf_op jit(solution)/shard_map/dot_general | solution.py:37
  16.6 74.5 %all-reduce.5.cloned.1.call-done = f32[4,256,1024]{2,1,0:T(8,128)} async-done(((f32[4,256,1024]{2,1,0:T(8,128)}), f32[4,256,1024]{2,1,0:T(8,128)}) %all-reduce.5.cloned.1.call-update) | async-done | bytes 4194320 | tf_op jit(solution)/shard_map/psum | solution.py:41
  91.1 2.1 convolution_bitcast_fusion.3
  93.2 1.9 copy.31
  95.2 74.4 %reduce-scatter.13.cloned.1.call-done = f32[32,1024]{1,0:T(8,128)} async-done(((f32[512,1024]{1,0:T(8,128)}), f32[32,1024]{1,0:T(8,128)}) %reduce-scatter.13.cloned.1.call-update) | async-done | bytes 131088 | tf_op jit(solution)/shard_map/reduce_scatter | solution.py:54
  169.5 0.9 convert_element_type.31
  170.6 18.4 %all_to_all.20 = bf16[16,32,1024]{2,1,0:T(8,128)(2,1)S(1)} all-to-all(bf16[16,32,1024]{2,1,0:T(8,128)(2,1)S(1)} %stack.6), channel_id=1, replica_groups=mesh['rows'=8,'cols'=16] {'cols'}, dimensions={0} | all-to-all | bytes 2097152 | tf_op jit(solution)/shard_map/all_to_all | solution.py:60
  188.9 2.4 convolution_bitcast_fusion.4
  191.4 61.7 %all-reduce.7.cloned.1.call-done = f32[256,1024]{1,0:T(8,128)} async-done(((f32[256,1024]{1,0:T(8,128)}), f32[256,1024]{1,0:T(8,128)}) %all-reduce.7.cloned.1.call-update) | async-done | bytes 1048592 | tf_op jit(solution)/shard_map/psum | solution.py:50
  253.1 2.5 convolution_bitcast_fusion.2
  255.6 1.9 copy.33
  257.5 73.8 %reduce-scatter.15.cloned.1.call-done = f32[32,1024]{1,0:T(8,128)} async-done(((f32[512,1024]{1,0:T(8,128)}), f32[32,1024]{1,0:T(8,128)}) %reduce-scatter.15.cloned.1.call-update) | async-done | bytes 131088 | tf_op jit(solution)/shard_map/reduce_scatter | solution.py:54
  331.3 0.9 convert_element_type.33
  332.3 18.5 %all_to_all.21 = bf16[16,32,1024]{2,1,0:T(8,128)(2,1)S(1)} all-to-all(bf16[16,32,1024]{2,1,0:T(8,128)(2,1)S(1)} %stack.7), channel_id=1, replica_groups=mesh['rows'=8,'cols'=16] {'cols'}, dimensions={0} | all-to-all | bytes 2097152 | tf_op jit(solution)/shard_map/all_to_all | solution.py:60
  350.8 1.4 fusion.35
  352.2 2.4 fusion.4
  354.7 61.7 %all-reduce.9.cloned.1.call-done = f32[256,1024]{1,0:T(8,128)} async-done(((f32[256,1024]{1,0:T(8,128)}), f32[256,1024]{1,0:T(8,128)}) %all-reduce.9.cloned.1.call-update) | async-done | bytes 1048592 | tf_op jit(solution)/shard_map/psum | solution.py:50
  416.4 3.8 convolution_bitcast_fusion.1
  420.2 2.9 copy.35
  423.2 73.8 %reduce-scatter.17.cloned.1.call-done = f32[32,1024]{1,0:T(8,128)} async-done(((f32[512,1024]{1,0:T(8,128)}), f32[32,1024]{1,0:T(8,128)}) %reduce-scatter.17.cloned.1.call-update) | async-done | bytes 131088 | tf_op jit(solution)/shard_map/reduce_scatter | solution.py:54
  498.0 18.3 %all_to_all.22 = bf16[16,32,1024]{2,1,0:T(8,128)(2,1)S(1)} all-to-all(bf16[16,32,1024]{2,1,0:T(8,128)(2,1)S(1)} %stack.8), channel_id=1, replica_groups=mesh['rows'=8,'cols'=16] {'cols'}, dimensions={0} | all-to-all | bytes 2097152 | tf_op jit(solution)/shard_map/all_to_all | solution.py:60
  516.4 1.4 fusion.31
  517.8 1.4 convolution_add_fusion.1
  519.3 2.4 fusion.3
  521.9 61.5 %all-reduce.11.cloned.1.call-done = f32[256,1024]{1,0:T(8,128)} async-done(((f32[256,1024]{1,0:T(8,128)}), f32[256,1024]{1,0:T(8,128)}) %all-reduce.11.cloned.1.call-update) | async-done | bytes 1048592 | tf_op jit(solution)/shard_map/psum | solution.py:50
  583.4 2.4 convolution_bitcast_fusion
  585.9 1.9 copy.37
  588.9 72.8 %reduce-scatter.19.cloned.1.call-done = f32[32,1024]{1,0:T(8,128)} async-done(((f32[512,1024]{1,0:T(8,128)}), f32[32,1024]{1,0:T(8,128)}) %reduce-scatter.19.cloned.1.call-update) | async-done | bytes 131088
  661.7 1.1 copy.38
  662.8 1.0 fusion.20
  664.4 27.9 %all_to_all.23 = f32[128,2,1024]{2,1,0:T(2,128)S(1)} all-to-all(f32[128,2,1024]{2,1,0:T(2,128)S(1)} %reshape.34), channel_id=1, replica_groups=mesh['rows'=8,'cols'=16] {'rows','cols'}, dimensions={0} | all-to-all | bytes 2097152 | tf_op jit(solution)/shard_map/all_to_all | solution.py:71
  692.3 1.7 reshape.35
  (38 shorter events, 3.5 us)
Async XLA Ops:
  6.5 84.6 %all-reduce.5.cloned.1.call-start = ((), (), s32[]{:S(2)}) async-start(), calls=%async_computation.8 | async-start | bytes 8388608 | tf_op jit(solution)/shard_map/psum | solution.py:41
  16.6 152.9 %reduce-scatter.13.cloned.1.call-start = ((), (), s32[]{:S(2)}) async-start(), calls=%async_computation.12 | async-start | bytes 2228224 | tf_op jit(solution)/shard_map/reduce_scatter | solution.py:54
  95.1 158.0 %all-reduce.7.cloned.1.call-start = ((), (), s32[]{:S(2)}) async-start(), calls=%async_computation.9 | async-start | bytes 2097152 | tf_op jit(solution)/shard_map/psum | solution.py:50
  191.3 139.9 %reduce-scatter.15.cloned.1.call-start = ((), (), s32[]{:S(2)}) async-start(), calls=%async_computation.13 | async-start | bytes 2228224 | tf_op jit(solution)/shard_map/reduce_scatter | solution.py:54
  257.5 159.0 %all-reduce.9.cloned.1.call-start = ((), (), s32[]{:S(2)}) async-start(), calls=%async_computation.10 | async-start | bytes 2097152 | tf_op jit(solution)/shard_map/psum | solution.py:50
  332.3 84.1 %copy-start = (bf16[4,256,512]{2,1,0:T(8,128)(2,1)S(1)}, bf16[4,256,512]{2,1,0:T(8,128)(2,1)}, u32[]{:S(2)}) copy-start(bf16[4,256,512]{2,1,0:T(8,128)(2,1)} %param.10) | copy-start | bytes 3145732
  354.7 142.3 %reduce-scatter.17.cloned.1.call-start = ((), (), s32[]{:S(2)}) async-start(), calls=%async_computation.14 | async-start | bytes 2228224 | tf_op jit(solution)/shard_map/reduce_scatter | solution.py:54
  423.1 160.3 %all-reduce.11.cloned.1.call-start = ((), (), s32[]{:S(2)}) async-start(), calls=%async_computation.11 | async-start | bytes 2097152 | tf_op jit(solution)/shard_map/psum | solution.py:50
  521.7 140.0 %reduce-scatter.19.cloned.1.call-start = ((), (), s32[]{:S(2)}) async-start(), calls=%async_computation.15 | async-start | bytes 2228224
  585.9 1.9 copy-start.4
  585.9 2.4 copy-start.1
  585.9 2.6 copy-start.2
  585.9 2.8 copy-start.3
Sparse Core Ops, SparseCore 0:
  16.7 74.4 all-reduce.4
  95.2 74.2 reduce-scatter.12
  191.5 61.5 all-reduce.6
  257.6 73.6 reduce-scatter.14
  354.8 61.5 all-reduce.8
  423.2 73.7 reduce-scatter.16
  521.8 61.5 all-reduce.10
  588.0 73.6 reduce-scatter.18
